TPU v7x, 512 devices: a whole 4x8x8 slice. The times are simulated.
512 devices in a mesh: dp: 32 (over y, z_hi), seq: 16 (over x, z_lo, core).
Axes of the slice: x: 4, y: 8, z: 8 (z_hi: 4, z_lo: 2; z = z_hi * 2 + z_lo), core: 2. Of those that a mesh axis runs over, the one named last changes fastest.
Arguments:
- queries: bfloat16 [32, 2048, 2048], P('dp', 'seq'), may hold values from -6 to 6
- grad_out: bfloat16 [32, 2048, 2048], P('dp', 'seq'), may hold values from -6 to 6
- encoded: bfloat16 [32, 32, 64, 896], P('dp', 'seq'), may hold values from -6 to 6
- kv_weight: bfloat16 [896, 4096], P(None, 'dp'), may hold values from -0.1875 to 0.1875
- neighbour_ids: int32 [32, 32, 2], P('dp', 'seq'), may hold values from 0 to 31, all different within a row
- slot_map: int32 [32, 32], P('dp'), may hold values from 0 to 31, each once within a row
Outputs:
- attended: bfloat16 [32, 2048, 2048], P('dp', 'seq')
- grad_queries: bfloat16 [32, 2048, 2048], P('dp', 'seq')
- grad_encoded: float32 [32, 32, 64, 896], P('dp', 'seq')
Inputs may be any that keep to these rules, and one draw needn't show every extreme that they name: `neighbour_ids`: each span names 2 different neighbour ids of its own sequence. `slot_map`: for each sequence a permutation; storage position p lies on the seq index p // 2.
All inputs are finite; a program needn't handle non-finite values.
Results may differ from a plain program's by a relative error of at most 0.018.
Values may be sent and summed in bfloat16 or wider, within the bound.
A program may use at most 64 MiB of HBM per device.

v0:
```python
import jax
import jax.numpy as jnp
from jax import lax
from jax.sharding import PartitionSpec as P

HEAD_SIZE = 128
HEADS = 16
SPAN = 64
NLEN = 64
READS = 2


def lookup_positions(neighbour_ids, slot_map):
    pool_size = slot_map.shape[1]
    matches = neighbour_ids[0][:, :, None] == jnp.arange(pool_size, dtype=jnp.int32)[None, None, :]
    positions = jnp.sum(jnp.where(matches, slot_map[0][None, None, :], 0), axis=2)
    return positions.reshape(-1)


def per_device(queries, grad_out, encoded, kv_weight, neighbour_ids, slot_map):
    hidden = HEADS * HEAD_SIZE
    scale_factor = HEAD_SIZE ** (-0.5)
    spans = queries.shape[1] // SPAN
    pool_size = slot_map.shape[1]
    width_enc = encoded.shape[3]
    flat_pos = lookup_positions(neighbour_ids, slot_map)
    read_count = flat_pos.shape[0]
    read_rows = read_count * NLEN
    pool_rows = lax.all_gather(encoded, "seq", axis=1, tiled=True)[0]
    picked = jnp.take(pool_rows, flat_pos, axis=0).reshape(read_rows, width_enc)
    whole_weight = lax.all_gather(kv_weight, "dp", axis=1, tiled=True)
    kv_flat = jnp.dot(picked, whole_weight, preferred_element_type=jnp.float32).astype(jnp.bfloat16)
    kv_spans = kv_flat.reshape(spans, READS * NLEN, 2 * hidden)
    keys = kv_spans[:, :, :hidden].reshape(spans, READS * NLEN, HEADS, HEAD_SIZE)
    values = kv_spans[:, :, hidden:].reshape(spans, READS * NLEN, HEADS, HEAD_SIZE)
    query_tiles = queries[0].reshape(spans, SPAN, HEADS, HEAD_SIZE)
    grad_tiles = grad_out[0].reshape(spans, SPAN, HEADS, HEAD_SIZE)
    scores = (
        jnp.einsum("cqhd,ckhd->chqk", query_tiles, keys, preferred_element_type=jnp.float32)
        * scale_factor
    )
    expos = jnp.exp(scores)
    probs = expos / jnp.sum(expos, axis=-1, keepdims=True)
    probs_low = probs.astype(jnp.bfloat16)
    attended = jnp.einsum("chqk,ckhd->cqhd", probs_low, values, preferred_element_type=jnp.float32)
    attended = attended.astype(jnp.bfloat16).reshape(1, spans * SPAN, hidden)
    d_probs = jnp.einsum("cqhd,ckhd->chqk", grad_tiles, values, preferred_element_type=jnp.float32)
    delta = jnp.sum(probs * d_probs, axis=-1, keepdims=True)
    d_scores = (probs * (d_probs - delta) * scale_factor).astype(jnp.bfloat16)
    grad_queries = jnp.einsum("chqk,ckhd->cqhd", d_scores, keys, preferred_element_type=jnp.float32)
    grad_queries = grad_queries.astype(jnp.bfloat16).reshape(1, spans * SPAN, hidden)
    d_keys = jnp.einsum(
        "chqk,cqhd->ckhd", d_scores, query_tiles, preferred_element_type=jnp.float32
    )
    d_values = jnp.einsum(
        "chqk,cqhd->ckhd", probs_low, grad_tiles, preferred_element_type=jnp.float32
    )
    grad_reads = jnp.concatenate(
        [d_keys.reshape(read_rows, hidden), d_values.reshape(read_rows, hidden)], axis=-1
    ).astype(jnp.bfloat16)
    enc_reads = lax.dot_general(
        grad_reads, whole_weight, (((1,), (1,)), ((), ())), preferred_element_type=jnp.float32
    )
    enc_reads = enc_reads.reshape(read_count, NLEN, width_enc)
    onehot = (flat_pos[:, None] == jnp.arange(pool_size, dtype=jnp.int32)[None, :]).astype(
        jnp.float32
    )
    partial_value = jnp.einsum("rn,rlk->nlk", onehot, enc_reads, precision=lax.Precision.HIGHEST)
    rounded = lax.optimization_barrier(partial_value.astype(jnp.bfloat16))
    grad_encoded = lax.psum_scatter(
        rounded.astype(jnp.float32)[None].astype(jnp.bfloat16),
        "seq",
        scatter_dimension=1,
        tiled=True,
    ).astype(jnp.float32)
    return (attended, grad_queries, grad_encoded)


def solution(mesh):
    in_specs = (
        P("dp", "seq", None),
        P("dp", "seq", None),
        P("dp", "seq", None, None),
        P(None, "dp"),
        P("dp", "seq", None),
        P("dp", None),
    )
    out_specs = (P("dp", "seq", None), P("dp", "seq", None), P("dp", "seq", None, None))
    return jax.shard_map(
        per_device, mesh=mesh, in_specs=in_specs, out_specs=out_specs, check_vma=False
    )
```

profile of v0, /device:TPU:16, one launch (start us, length us, event | category | flops | bytes accessed | tf_op | source)
XLA Modules:
  0.0 315.2 jit_solution(13738438806581832548)
XLA Ops:
  7.2 0.0 all-gather.3.cloned.1.call-start
  7.2 0.7 all-gather.3.cloned.1.call-update
  7.9 0.0 all-gather.5.cloned.1.call-start
  7.9 0.7 all-gather.5.cloned.1.call-update
  8.6 0.0 reduce-scatter.2.cloned.1.call-start
  8.7 0.9 fusion.30
  9.6 0.1 reshape.81
  9.7 0.1 reshape.80
  9.8 0.1 broadcast_in_dim.36
  9.9 0.1 broadcast_in_dim.37
  9.9 1.2 copy.73
  11.1 1.1 copy.74
  12.3 44.6 %all-gather.3.cloned.1.call-done = bf16[1,32,64,896]{3,2,0,1:T(8,128)(2,1)} async-done(((bf16[1,2,64,896]{3,2,0,1:T(8,128)(2,1)}), bf16[1,32,64,896]{3,2,0,1:T(8,128)(2,1)}) %all-gather.3.cloned.1.call-update) | async-done | bytes 3670032 | tf_op jit(solution)/shard_map/all_gather | solution.py:29
  56.8 2.7 gather_fusion
  59.5 0.1 bitcast_select_fusion
  59.6 140.9 %all-gather.5.cloned.1.call-done = bf16[896,4096]{1,0:T(8,128)(2,1)} async-done(((bf16[896,128]{1,0:T(8,128)(2,1)}), bf16[896,4096]{1,0:T(8,128)(2,1)}) %all-gather.5.cloned.1.call-update) | async-done | bytes 7340048 | tf_op jit(solution)/shard_map/all_gather | solution.py:31
  200.5 5.4 %convolution_convert_fusion = bf16[256,4096]{1,0:T(8,128)(2,1)S(1)} fusion(bf16[256,896]{1,0:T(8,128)(2,1)S(1)} %bitcast_select_fusion, bf16[896,4096]{1,0:T(8,128)(2,1)} %all-gather.5.cloned.1.call-done), kind=kOutput, calls=%fused_computation.2 | convolution fusion | flops 1880096768 | bytes 9895936 | tf_op jit(solution)/shard_map/dot_general | solution.py:32
  206.0 1.3 fusion.42
  207.2 0.7 copy.71
  207.9 0.0 copy-start
  207.9 2.0 copy.72
  209.9 0.4 fusion.11
  210.3 0.0 copy-start.2
  210.3 1.1 copy-done.2
  211.4 1.3 fusion.23
  212.7 3.5 %fusion.6 = bf16[2,128,16,128]{3,1,2,0:T(8,128)(2,1)} fusion(bf16[2,64,16,128]{3,2,1,0:T(8,128)(2,1)S(1)} %bitcast.70, f32[2,16,64,128]{3,2,1,0:T(8,128)} %copy-done.2), kind=kOutput, calls=%fused_computation.11 | convolution fusion | flops 68159616 | bytes 2621440 | tf_op jit(solution)/shard_map/chqk,cqhd->ckhd/dot_general | solution.py:55
  216.2 0.0 copy-done
  216.2 1.4 convolution_bitcast_fusion
  217.6 3.0 copy.63
  220.6 2.9 fusion.5
  223.5 0.7 copy.61
  224.2 1.7 copy_bitcast_fusion
  225.9 5.7 %fusion.1 = f32[256,896]{1,0:T(8,128)S(1)} fusion(bf16[896,4096]{1,0:T(8,128)(2,1)} %all-gather.5.cloned.1.call-done, bf16[256,2048]{1,0:T(8,128)(2,1)S(1)} %get-tuple-element.17, bf16[256,2048]{1,0:T(8,128)(2,1)S(1)} %get-tuple-element.18), kind=kOutput, calls=%fused_computation.4 | convolution fusion | flops 1883242496 | bytes 10354688 | tf_op jit(solution)/shard_map/dot_general | solution.py:61
  231.6 3.8 %convolution_convert_fusion.1 = bf16[32,64,896]{2,0,1:T(8,128)(2,1)S(1)} fusion(f32[4,64,896]{2,1,0:T(8,128)S(1)} %bitcast.73, s32[4]{0:T(128)S(1)} %reshape.80), kind=kOutput, calls=%fused_computation.3 | convolution fusion | flops 89915520 | bytes 4587536 | tf_op jit(solution)/shard_map/rn,rlk->nlk/dot_general | solution.py:68
  235.4 3.1 copy.65
  238.5 0.0 copy-start.1
  238.5 0.0 reduce-scatter.2.cloned.1.call-update
  238.5 1.2 copy-done.1
  239.7 2.6 fusion.13
  242.3 0.3 copy.55
  242.6 1.0 reshape.85
  243.6 3.0 fusion.14
  246.7 0.3 copy.59
  247.0 1.0 reshape.86
  248.0 58.8 %reduce-scatter.2.cloned.1.call-done = bf16[1,2,64,896]{3,2,0,1:T(8,128)(2,1)} async-done(((bf16[1,32,64,896]{3,2,0,1:T(8,128)(2,1)}), bf16[1,2,64,896]{3,2,0,1:T(8,128)(2,1)}) %reduce-scatter.2.cloned.1.call-update) | async-done | bytes 229392 | tf_op jit(solution)/shard_map/reduce_scatter | solution.py:70
  306.9 1.7 bitcast_convert_fusion
  (3 shorter events, 0.0 us)
Async XLA Ops:
  7.2 49.7 %all-gather.3.cloned.1.call-start = ((), (), s32[]{:S(2)}) async-start(), calls=%async_computation.1 | async-start | bytes 3899392 | tf_op jit(solution)/shard_map/all_gather | solution.py:29
  7.9 192.7 %all-gather.5.cloned.1.call-start = ((), (), s32[]{:S(2)}) async-start(), calls=%async_computation.2 | async-start | bytes 7569408 | tf_op jit(solution)/shard_map/all_gather | solution.py:31
  8.6 298.2 %reduce-scatter.2.cloned.1.call-start = ((), (), s32[]{:S(2)}) async-start(), calls=%async_computation.3 | async-start | bytes 3899392 | tf_op jit(solution)/shard_map/reduce_scatter | solution.py:70
  207.9 8.3 %copy-start = (bf16[2,128,2048]{1,2,0:T(8,128)(2,1)}, bf16[2,128,2048]{1,2,0:T(8,128)(2,1)S(1)}, u32[]{:S(2)}) copy-start(bf16[2,128,2048]{1,2,0:T(8,128)(2,1)S(1)} %copy.71) | copy-start | bytes 3145732
  210.3 1.1 copy-start.2
  238.5 1.2 copy-start.1
Sparse Core Ops, SparseCore 0:
  10.1 46.6 all-gather.2
  59.9 140.6 all-gather.4
  238.6 68.2 reduce-scatter.1
where the time goes:
time: 316 us; the launch traced here: 315 us
  waiting for transfers between devices  246 us (78%)
  matrix products  28.7 us (9%)
  local copies, waits for them, and re-layouts  22.6 us (7%)
  between operations  13.9 us (4%)
  other arithmetic  4.12 us (1%)
    all_gather x1, waiting for transfers between devices, per_device(): whole_weight = lax.all_gather(kv_weight, 'dp', axis=1, tiled=True)  141 us
    reduce_scatter x1, waiting for transfers between devices, per_device(): lax.psum_scatter(rounded.astype(jnp.float32)[None].astype(jnp.bfloat16),...  58.8 us
    all_gather x1, waiting for transfers between devices, per_device(): pool_rows = lax.all_gather(encoded, 'seq', axis=1, tiled=True)[0]  44.6 us
    unnamed x10, local copies, waits for them, and re-layouts  7.21 us
  transfers between devices with their start and end apart: 3, of which 3 were waited for; matrix products, arithmetic and copies ran while one was open for 5% of the time, Pallas kernels for 0%

commit v1 on v0

--- a/solution.py
+++ b/solution.py
@@ -28,7 +28,10 @@
     read_rows = read_count * NLEN
     pool_rows = lax.all_gather(encoded, "seq", axis=1, tiled=True)[0]
     picked = jnp.take(pool_rows, flat_pos, axis=0).reshape(read_rows, width_enc)
-    whole_weight = lax.all_gather(kv_weight, "dp", axis=1, tiled=True)
+    size = lax.axis_size("dp")
+    pieces = jnp.stack([kv_weight for _ in range(size)])
+    pieces = lax.all_to_all(pieces, "dp", split_axis=0, concat_axis=0)
+    whole_weight = jnp.concatenate(pieces, axis=1)
     kv_flat = jnp.dot(picked, whole_weight, preferred_element_type=jnp.float32).astype(jnp.bfloat16)
     kv_spans = kv_flat.reshape(spans, READS * NLEN, 2 * hidden)
     keys = kv_spans[:, :, :hidden].reshape(spans, READS * NLEN, HEADS, HEAD_SIZE)

time: 316 us -> 388 us (1.23)
  the two profiles are of different devices: /device:TPU:16 before, /device:TPU:8 now
where the time goes in v1:
time: 388 us
  waiting for transfers between devices  298 us (77%)
  matrix products  28.8 us (7%)
  local copies, waits for them, and re-layouts  26.6 us (7%)
  starting transfers between devices  16.4 us (4%)
  between operations  14.2 us (4%)
    all_gather x1, waiting for transfers between devices, per_device(): pool_rows = lax.all_gather(encoded, 'seq', axis=1, tiled=True)[0]  214 us
    reduce_scatter x1, waiting for transfers between devices, per_device(): lax.psum_scatter(rounded.astype(jnp.float32)[None].astype(jnp.bfloat16),...  83.5 us
    all_to_all x1, starting transfers between devices, per_device(): pieces = lax.all_to_all(pieces, 'dp', split_axis=0, concat_axis=0)  16.4 us
  transfers between devices with their start and end apart: 3, of which 2 were waited for; matrix products, arithmetic and copies ran while one was open for 3% of the time, Pallas kernels for 0%

profile of v1, /device:TPU:8, one launch (start us, length us, event | category | flops | bytes accessed | tf_op | source)
XLA Modules:
  0.0 387.8 jit_solution(10796559772806150468)
XLA Ops:
  7.2 1.1 copy.51
  8.3 4.1 %stack.2 = bf16[32,896,128]{1,2,0:T(8,128)(2,1)} broadcast(bf16[896,128]{0,1:T(8,128)(2,1)S(1)} %copy.51), dimensions={1,2} | broadcast | bytes 7569408 | tf_op jit(solution)/shard_map/stack | solution.py:32
  12.3 0.0 copy-start.5
  12.3 0.0 copy-start.6
  12.3 0.0 copy-start.3
  12.3 0.0 copy-start.4
  12.3 16.4 %all-to-all-start = ((bf16[32,896,128]{1,2,0:T(8,128)(2,1)}), bf16[32,896,128]{1,2,0:T(8,128)(2,1)}, u32[]{:S(2)}, u32[]{:S(2)}) async-start(bf16[32,896,128]{1,2,0:T(8,128)(2,1)} %stack.2), calls=%async_computation | async-start | bytes 14680064 | tf_op jit(solution)/shard_map/all_to_all | solution.py:33
  28.7 0.0 all-gather.2.cloned.1.call-start
  28.8 0.7 all-gather.2.cloned.1.call-update
  29.5 0.0 reduce-scatter.2.cloned.1.call-start
  29.5 0.0 copy-done.5
  29.5 0.0 copy-done.6
  29.5 0.2 fusion.30
  29.7 0.1 reshape.118
  29.8 0.1 reshape.117
  29.9 0.0 copy-done.3
  29.9 0.1 copy.78
  30.0 0.0 copy-done.4
  30.0 0.1 copy.79
  30.2 214.0 %all-gather.2.cloned.1.call-done = bf16[1,32,64,896]{3,2,0,1:T(8,128)(2,1)} async-done(((bf16[1,2,64,896]{3,2,0,1:T(8,128)(2,1)}), bf16[1,32,64,896]{3,2,0,1:T(8,128)(2,1)}) %all-gather.2.cloned.1.call-update) | async-done | bytes 3670032 | tf_op jit(solution)/shard_map/all_gather | solution.py:29
  244.2 2.7 gather_fusion
  246.9 0.1 broadcast_select_fusion
  247.0 0.0 all-to-all-done
  247.0 5.4 %convolution_convert_fusion = bf16[256,4096]{1,0:T(8,128)(2,1)S(1)} fusion(bf16[256,896]{1,0:T(8,128)(2,1)S(1)} %bitcast.72, bf16[896,4096]{0,1:T(8,128)(2,1)} %bitcast.7), kind=kOutput, calls=%fused_computation.2 | convolution fusion | flops 1880096768 | bytes 9895936 | tf_op jit(solution)/shard_map/dot_general | solution.py:35
  252.5 1.3 fusion.42
  253.7 0.7 copy.76
  254.4 0.0 copy-start
  254.4 2.0 copy.77
  256.4 0.4 fusion.11
  256.8 0.0 copy-start.2
  256.8 1.1 copy-done.2
  257.9 1.3 fusion.23
  259.2 3.5 fusion.6
  262.7 0.0 copy-done
  262.7 1.4 convolution_bitcast_fusion
  264.1 1.9 copy.65
  266.0 1.3 concatenate.10
  267.3 2.9 fusion.5
  270.2 1.7 copy.63
  272.0 1.5 concatenate.9
  273.5 5.8 %fusion.1 = f32[4,64,896]{2,1,0:T(8,128)S(1)} fusion(bf16[896,4096,1]{0,1,2:T(8,128)(2,1)} %bitcast.19, bf16[4,64,2048]{2,1,0:T(8,128)(2,1)} %concatenate.10, bf16[4,64,2048]{2,1,0:T(8,128)(2,1)S(1)} %concatenate.9), kind=kOutput, calls=%fused_computation.4 | convolution fusion | flops 1883242496 | bytes 10354688 | tf_op jit(solution)/shard_map/dot_general | solution.py:64
  279.2 3.8 convolution_convert_fusion.1
  283.0 3.1 copy.68
  286.1 0.0 copy-start.1
  286.1 0.0 reduce-scatter.2.cloned.1.call-update
  286.1 1.2 copy-done.1
  287.3 2.6 fusion.13
  289.9 0.3 copy.57
  290.2 1.0 reshape.124
  291.3 3.0 fusion.14
  294.3 0.3 copy.61
  294.6 1.0 reshape.125
  295.7 83.5 %reduce-scatter.2.cloned.1.call-done = bf16[1,2,64,896]{3,2,0,1:T(8,128)(2,1)} async-done(((bf16[1,32,64,896]{3,2,0,1:T(8,128)(2,1)}), bf16[1,2,64,896]{3,2,0,1:T(8,128)(2,1)}) %reduce-scatter.2.cloned.1.call-update) | async-done | bytes 229392 | tf_op jit(solution)/shard_map/reduce_scatter | solution.py:73
  379.2 1.7 bitcast_convert_fusion
  (3 shorter events, 0.0 us)
Async XLA Ops:
  12.3 17.2 %copy-start.5 = (s32[1,2,2]{2,1,0:T(2,128)S(1)}, s32[1,2,2]{2,1,0:T(2,128)}, u32[]{:S(2)}) copy-start(s32[1,2,2]{2,1,0:T(2,128)} %param.10) | copy-start | bytes 52
  12.3 17.2 %copy-start.6 = (s32[1,32]{1,0:T(1,128)S(1)}, s32[1,32]{1,0:T(1,128)}, u32[]{:S(2)}) copy-start(s32[1,32]{1,0:T(1,128)} %param.11) | copy-start | bytes 388
  12.3 17.6 %copy-start.3 = (bf16[1,128,2048]{2,1,0:T(8,128)(2,1)S(1)}, bf16[1,128,2048]{2,1,0:T(8,128)(2,1)}, u32[]{:S(2)}) copy-start(bf16[1,128,2048]{2,1,0:T(8,128)(2,1)} %param.6) | copy-start | bytes 1572868
  12.3 17.7 %copy-start.4 = (bf16[1,128,2048]{2,1,0:T(8,128)(2,1)S(1)}, bf16[1,128,2048]{2,1,0:T(8,128)(2,1)}, u32[]{:S(2)}) copy-start(bf16[1,128,2048]{2,1,0:T(8,128)(2,1)} %param.7) | copy-start | bytes 1572868
  12.3 234.6 %all-to-all-start = ((bf16[32,896,128]{1,2,0:T(8,128)(2,1)}), bf16[32,896,128]{1,2,0:T(8,128)(2,1)}, u32[]{:S(2)}, u32[]{:S(2)}) async-start(bf16[32,896,128]{1,2,0:T(8,128)(2,1)} %stack.2), calls=%async_computation | async-start | bytes 14680064 | tf_op jit(solution)/shard_map/all_to_all | solution.py:33
  28.7 215.5 %all-gather.2.cloned.1.call-start = ((), (), s32[]{:S(2)}) async-start(), calls=%async_computation.2 | async-start | bytes 3899392 | tf_op jit(solution)/shard_map/all_gather | solution.py:29
  29.5 349.7 %reduce-scatter.2.cloned.1.call-start = ((), (), s32[]{:S(2)}) async-start(), calls=%async_computation.3 | async-start | bytes 3899392 | tf_op jit(solution)/shard_map/reduce_scatter | solution.py:73
  254.4 8.3 %copy-start = (bf16[2,128,2048]{1,2,0:T(8,128)(2,1)}, bf16[2,128,2048]{1,2,0:T(8,128)(2,1)S(1)}, u32[]{:S(2)}) copy-start(bf16[2,128,2048]{1,2,0:T(8,128)(2,1)S(1)} %copy.76) | copy-start | bytes 3145732
  256.8 1.1 copy-start.2
  286.1 1.2 copy-start.1
Sparse Core Ops, SparseCore 0:
  31.7 212.4 all-gather.1
  286.2 92.9 reduce-scatter.1
